TPU v7x, 256 devices: a whole 4x4x8 slice. The times are simulated.
256 devices in a mesh: dp: 8 (over x, z_hi), pipe: 4 (over z_lo), expert: 8 (over y, core).
Axes of the slice: x: 4, y: 4, z: 8 (z_hi: 2, z_lo: 4; z = z_hi * 4 + z_lo), core: 2. Of those that a mesh axis runs over, the one named last changes fastest.
Arguments:
- tokens: bfloat16 [8192, 2048], P(('dp', 'expert')), may hold values from -6 to 6
- cotangent: bfloat16 [8192, 2048], P(('dp', 'expert')), may hold values from -6 to 6
- owner_ids: int32 [4, 8192, 4], P('pipe', ('dp', 'expert')), may hold values from 0 to 63, all different within a row; in each aligned block of 32 rows (0 to 31, 32 to 63, ..., all dimensions but the last counted through in order) at most 3 rows name the same one
- gate_weights: bfloat16 [4, 8192, 4], P('pipe', ('dp', 'expert')), may hold values from 0.049804688 to 0.25
- norm_gain: float32 [4, 2048], P('pipe'), may hold values from 0.5 to 1.5
- w_gate: bfloat16 [4, 64, 2048, 384], P('pipe', ('dp', 'expert')), may hold values from -0.125 to 0.125
- w_up: bfloat16 [4, 64, 2048, 384], P('pipe', ('dp', 'expert')), may hold values from -0.125 to 0.125
- w_down: bfloat16 [4, 64, 384, 2048], P('pipe', ('dp', 'expert')), may hold values from -0.3125 to 0.3125
Outputs:
- segment_out: bfloat16 [4, 8192, 2048], P('pipe', ('dp', 'expert'))
- segment_grad: bfloat16 [4, 8192, 2048], P('pipe', ('dp', 'expert'))
- gain_grad: float32 [4, 2048], P('pipe')
Inputs may be any that keep to these rules, and one draw needn't show every extreme that they name: `owner_ids`: each row names 4 different owners. In each aligned block of 32 rows (layers in order, then tokens) no owner is named by more than 3 rows, and that bound is reached.
All inputs are finite; a program needn't handle non-finite values.
Results may differ from a plain program's by a relative error of at most 0.014.
Values may be sent and summed in bfloat16 or wider, within the bound.
A program may use at most 128 MiB of HBM per device.

v0:
```python
import jax
import jax.numpy as jnp
from jax import lax
from jax.sharding import PartitionSpec as P

MICRO = 4
epsilon = 1e-06


def from_behind(value, axis, steps):
    count = lax.axis_size(axis)
    leading, last = (max(0, -steps), min(count, count - steps))
    return lax.ppermute(value, axis, [(source, source + steps) for source in range(leading, last)])


def inverse_rms(values):
    return lax.rsqrt(jnp.mean(values * values, axis=-1, keepdims=True) + epsilon)


def contract_last(left, right):
    return lax.dot_general(
        left, right, (((1,), (1,)), ((), ())), preferred_element_type=jnp.float32
    )


def route_tables(ids_part, owners, capacity):
    owner_range = jnp.arange(owners, dtype=jnp.int32)
    onehot = (ids_part[:, :, None] == owner_range[None, None, :]).astype(jnp.int32)
    member = jnp.sum(onehot, axis=1)
    position = jnp.cumsum(member, axis=0) - member
    slot_range = jnp.arange(capacity, dtype=jnp.int32)
    placed = (position[:, :, None] == slot_range[None, None, :]) & (member[:, :, None] > 0)
    placing = jnp.transpose(placed, (1, 2, 0)).astype(jnp.bfloat16)
    return (onehot.astype(jnp.float32), placing)


def gate_slots(onehot, gates_part, placing, experts_here):
    gate_pairs = gates_part.astype(jnp.float32).reshape(gates_part.shape[0], -1, experts_here)
    chosen = jnp.einsum("rjo,rjc->roc", onehot, gate_pairs)
    return jnp.einsum("okr,roc->okc", placing.astype(jnp.float32), chosen).astype(jnp.bfloat16)


def send_rows(row_block, pair_block):
    got_rows, got_pairs = (
        lax.all_to_all(row_block, ("dp", "expert"), split_axis=0, concat_axis=0, tiled=True),
        lax.all_to_all(pair_block, ("dp", "expert"), split_axis=0, concat_axis=0, tiled=True),
    )
    return (got_rows, got_pairs)


def return_rows(row_block):
    return lax.all_to_all(row_block, ("dp", "expert"), split_axis=0, concat_axis=0, tiled=True)


def send_grads(row_block):
    return lax.all_to_all(row_block, ("dp", "expert"), split_axis=0, concat_axis=0, tiled=True)


def return_grads(row_block):
    return lax.all_to_all(row_block, ("dp", "expert"), split_axis=0, concat_axis=0, tiled=True)


def expert_forward(flat_rows, flat_pairs, joint_mats, down_mats):
    hidden_width = down_mats.shape[1]
    joint_pre = jnp.dot(flat_rows, joint_mats[0], preferred_element_type=jnp.float32)
    gate_pre = joint_pre[:, :hidden_width]
    up_pre = joint_pre[:, hidden_width:]
    hidden = (jax.nn.silu(gate_pre) * up_pre).astype(jnp.bfloat16)
    projected = jnp.dot(hidden, down_mats[0], preferred_element_type=jnp.float32)
    term = flat_pairs.astype(jnp.float32) * projected
    kept_both = [joint_pre]
    return (term.astype(jnp.bfloat16), jnp.stack(kept_both))


def expert_backward(grad_rows, flat_pairs, joint_keep, joint_mats, down_mats):
    hidden_width = down_mats.shape[1]
    q_vals = contract_last(grad_rows, down_mats[0])
    gate_pre = joint_keep[0][:, :hidden_width]
    up_pre = joint_keep[0][:, hidden_width:]
    sigma = jax.nn.sigmoid(gate_pre)
    weight = flat_pairs.astype(jnp.float32)
    d_gate = (q_vals * weight * up_pre * sigma * (1.0 + gate_pre * (1.0 - sigma))).astype(
        jnp.bfloat16
    )
    d_up = (q_vals * weight * gate_pre * sigma).astype(jnp.bfloat16)
    joint_grad = jnp.concatenate([d_gate, d_up], axis=1)
    term = contract_last(joint_grad, joint_mats[0])
    return term.astype(jnp.bfloat16)


def body(tokens, cotangent, owner_ids, gate_weights, norm_gain, w_gate, w_up, w_down):
    segments = lax.axis_size("pipe")
    segment_index = lax.axis_index("pipe")
    owners = lax.axis_size("dp") * lax.axis_size("expert")
    tok_rows = tokens.shape[0]
    width = tokens.shape[1]
    micro_rows = tok_rows // MICRO
    route_count = owner_ids.shape[2]
    capacity = max(2, (5 * micro_rows * route_count + 4 * owners - 1) // (4 * owners))
    slot_count = owners * capacity
    gain_row = norm_gain[0]
    joint_mats = jnp.concatenate([w_gate[0], w_up[0]], axis=2)
    down_mats = w_down[0]
    layer_ids = owner_ids[0]
    layer_gates = gate_weights[0]
    experts_here = joint_mats.shape[0]
    joint_width = joint_mats.shape[2]

    def skip_forward(operands):
        return (
            jnp.zeros((slot_count, width), jnp.bfloat16),
            jnp.zeros((experts_here, slot_count, joint_width), jnp.float32),
        )

    def run_forward(operands):
        return expert_forward(operands[0], operands[1], joint_mats, down_mats)

    def skip_backward(operands):
        return jnp.zeros((slot_count, width), jnp.bfloat16)

    def run_backward(operands):
        return expert_backward(operands[0], operands[1], operands[2], joint_mats, down_mats)

    def timing(micro):
        is_valid = (micro >= 0) & (micro < MICRO)
        slot_pick = jnp.where(is_valid, micro, MICRO)
        start_row = jnp.clip(micro, 0, MICRO - 1) * micro_rows
        return (is_valid, slot_pick, start_row)

    layer_outs = jnp.zeros((MICRO + 1, micro_rows, width), jnp.bfloat16)
    layer_ins = jnp.zeros((MICRO + 1, micro_rows, width), jnp.bfloat16)
    kept_joint = jnp.zeros((MICRO + 1, experts_here, slot_count, joint_width), jnp.float32)
    kept_pairs = jnp.zeros((MICRO + 1, slot_count, experts_here), jnp.bfloat16)
    grad_outs = jnp.zeros((MICRO + 1, micro_rows, width), jnp.bfloat16)
    gain_sum = jnp.zeros((width,), jnp.float32)
    ticks = MICRO + segments - 1
    incoming = jnp.zeros((micro_rows, width), jnp.bfloat16)
    for tick_num in range(ticks):
        forward_is_valid, forward_slot_pick, forward_start_row = timing(tick_num - segment_index)
        forward_own_part = lax.dynamic_slice_in_dim(tokens, forward_start_row, micro_rows, 0)
        forward_layer_in = jnp.where(segment_index == 0, forward_own_part, incoming)
        forward_ids_part = lax.dynamic_slice_in_dim(layer_ids, forward_start_row, micro_rows, 0)
        gates_part = lax.dynamic_slice_in_dim(layer_gates, forward_start_row, micro_rows, 0)
        forward_x_float = forward_layer_in.astype(jnp.float32)
        forward_scale = inverse_rms(forward_x_float)
        normed = (forward_x_float * forward_scale * gain_row).astype(jnp.bfloat16)
        forward_onehot, forward_placing = route_tables(forward_ids_part, owners, capacity)
        row_block = jnp.einsum(
            "okr,rd->okd", forward_placing, normed, preferred_element_type=jnp.float32
        ).astype(jnp.bfloat16)
        pair_block = gate_slots(forward_onehot, gates_part, forward_placing, experts_here)
        f_valid, f_pick, layer_in, x_float, f_placing, row_block, pair_block = (
            forward_is_valid,
            forward_slot_pick,
            forward_layer_in,
            forward_x_float,
            forward_placing,
            row_block,
            pair_block,
        )
        got_rows, got_pairs = send_rows(row_block, pair_block)
        flat_rows = got_rows.reshape(slot_count, width)
        flat_pairs = got_pairs.reshape(slot_count, experts_here)
        result, joint_pre = lax.cond(f_valid, run_forward, skip_forward, (flat_rows, flat_pairs))
        returned = return_rows(result.reshape(owners, capacity, width))
        branch = jnp.einsum("okr,okd->rd", f_placing, returned, preferred_element_type=jnp.float32)
        layer_out = (x_float + branch).astype(jnp.bfloat16)
        layer_outs = lax.dynamic_update_index_in_dim(layer_outs, layer_out, f_pick, 0)
        layer_ins = lax.dynamic_update_index_in_dim(layer_ins, layer_in, f_pick, 0)
        kept_joint = lax.dynamic_update_index_in_dim(kept_joint, joint_pre, f_pick, 0)
        kept_pairs = lax.dynamic_update_index_in_dim(kept_pairs, flat_pairs, f_pick, 0)
        if tick_num + 1 < ticks:
            incoming = from_behind(layer_out, "pipe", 1)
    incoming = jnp.zeros((micro_rows, width), jnp.bfloat16)
    for tick_num in range(ticks):
        backward_is_valid, backward_slot_pick, backward_start_row = timing(
            tick_num - (segments - 1 - segment_index)
        )
        own_part = lax.dynamic_slice_in_dim(cotangent, backward_start_row, micro_rows, 0)
        backward_grad_in = jnp.where(segment_index == segments - 1, own_part, incoming)
        ids_part = lax.dynamic_slice_in_dim(layer_ids, backward_start_row, micro_rows, 0)
        backward_layer_in = lax.dynamic_index_in_dim(
            layer_ins, backward_slot_pick, 0, keepdims=False
        )
        backward_x_float = backward_layer_in.astype(jnp.float32)
        backward_scale = inverse_rms(backward_x_float)
        onehot, backward_placing = route_tables(ids_part, owners, capacity)
        grad_block = jnp.einsum(
            "okr,rd->okd", backward_placing, backward_grad_in, preferred_element_type=jnp.float32
        ).astype(jnp.bfloat16)
        b_valid, b_pick, grad_in, bx_float, b_scale, b_placing, grad_block = (
            backward_is_valid,
            backward_slot_pick,
            backward_grad_in,
            backward_x_float,
            backward_scale,
            backward_placing,
            grad_block,
        )
        got_grads = send_grads(grad_block).reshape(slot_count, width)
        joint_keep = lax.dynamic_index_in_dim(kept_joint, b_pick, 0, keepdims=False)
        pair_keep = lax.dynamic_index_in_dim(kept_pairs, b_pick, 0, keepdims=False)
        owner_grad = lax.cond(
            b_valid, run_backward, skip_backward, (got_grads, pair_keep, joint_keep)
        )
        returned = return_grads(owner_grad.reshape(owners, capacity, width))
        normed_grad = jnp.einsum(
            "okr,okd->rd", b_placing, returned, preferred_element_type=jnp.float32
        )
        weighted = gain_row * normed_grad
        grad_x = (
            grad_in.astype(jnp.float32)
            + b_scale * weighted
            - bx_float
            * b_scale
            * b_scale
            * b_scale
            * jnp.mean(weighted * bx_float, axis=-1, keepdims=True)
        )
        gain_term = jnp.where(b_valid, jnp.sum(normed_grad * bx_float * b_scale, axis=0), 0.0)
        grad_bf, gain_term = (grad_x.astype(jnp.bfloat16), gain_term)
        grad_outs = lax.dynamic_update_index_in_dim(grad_outs, grad_bf, b_pick, 0)
        gain_sum = gain_sum + gain_term
        if tick_num + 1 < ticks:
            incoming = from_behind(grad_bf, "pipe", -1)
    gain_grad = lax.psum(gain_sum, ("dp", "expert"))
    segment_out = layer_outs[:MICRO].reshape(1, tok_rows, width)
    segment_grad = grad_outs[:MICRO].reshape(1, tok_rows, width)
    return (segment_out, segment_grad, gain_grad.reshape(1, width))


def solution(mesh):
    in_specs = (
        P(("dp", "expert"), None),
        P(("dp", "expert"), None),
        P("pipe", ("dp", "expert"), None),
        P("pipe", ("dp", "expert"), None),
        P("pipe", None),
        P("pipe", ("dp", "expert"), None, None),
        P("pipe", ("dp", "expert"), None, None),
        P("pipe", ("dp", "expert"), None, None),
    )
    out_specs = (
        P("pipe", ("dp", "expert"), None),
        P("pipe", ("dp", "expert"), None),
        P("pipe", None),
    )
    return jax.shard_map(body, mesh=mesh, in_specs=in_specs, out_specs=out_specs, check_vma=False)
```

profile of v0, /device:TPU:1, one launch (start us, length us, event | category | flops | bytes accessed | tf_op | source)
XLA Modules:
  0.0 1507.8 jit_solution(17595029229092546663)
XLA Ops:
  5.5 15.6 %all-to-all-start = ((bf16[64,3,1]{1,2,0:T(2,128)(2,1)}), bf16[64,3,1]{1,2,0:T(2,128)(2,1)S(1)}, u32[]{:S(2)}, u32[]{:S(2)}) async-start(bf16[64,3,1]{1,2,0:T(2,128)(2,1)} %copy.214), calls=%async_computation | async-start | bytes 65536 | tf_op jit(solution)/shard_map/all_to_all | solution.py:46
  40.4 25.5 %all-to-all-done.1 = bf16[64,3,2048]{2,1,0:T(4,128)(2,1)} async-done(((bf16[64,3,2048]{2,1,0:T(4,128)(2,1)}), bf16[64,3,2048]{2,1,0:T(4,128)(2,1)}, u32[]{:S(2)}, u32[]{:S(2)}) %all-to-all-start.1) | async-done | bytes 786464 | tf_op jit(solution)/shard_map/all_to_all | solution.py:45
  84.8 18.1 %all-to-all-done.2 = bf16[64,3,2048]{2,1,0:T(4,128)(2,1)} async-done(((bf16[64,3,2048]{2,1,0:T(4,128)(2,1)}), bf16[64,3,2048]{2,1,0:T(4,128)(2,1)}, u32[]{:S(2)}, u32[]{:S(2)}) %all-to-all-start.2) | async-done | bytes 786464 | tf_op jit(solution)/shard_map/all_to_all | solution.py:52
  122.4 14.5 all-to-all-start.4
  136.9 28.5 %all-to-all-done.4 = bf16[64,3,2048]{2,1,0:T(4,128)(2,1)} async-done(((bf16[64,3,2048]{2,1,0:T(4,128)(2,1)}), bf16[64,3,2048]{2,1,0:T(4,128)(2,1)}, u32[]{:S(2)}, u32[]{:S(2)}) %all-to-all-start.4) | async-done | bytes 786464 | tf_op jit(solution)/shard_map/all_to_all | solution.py:45
  184.1 18.4 %all-to-all-done.5 = bf16[64,3,2048]{2,1,0:T(4,128)(2,1)} async-done(((bf16[64,3,2048]{2,1,0:T(4,128)(2,1)}), bf16[64,3,2048]{2,1,0:T(4,128)(2,1)}, u32[]{:S(2)}, u32[]{:S(2)}) %all-to-all-start.5) | async-done | bytes 786464 | tf_op jit(solution)/shard_map/all_to_all | solution.py:52
  205.4 17.4 %collective-permute-start.1 = (bf16[32,2048]{1,0:T(8,128)(2,1)S(1)}, bf16[32,2048]{1,0:T(8,128)(2,1)S(1)}, u32[]{:S(2)}, u32[]{:S(2)}) collective-permute-start(bf16[32,2048]{1,0:T(8,128)(2,1)S(1)} %get-tuple-element.841), channel_id=1, source_target_pairs={{0,8},{8,16},{16,24},{1,9},{9,17},{17,25},{2,10},{10,18},{18,26},{... | collective-permute-start | bytes 393224 | tf_op jit(solution)/shard_map/ppermute | solution.py:13
  246.7 28.6 %all-to-all-done.7 = bf16[64,3,2048]{2,1,0:T(4,128)(2,1)} async-done(((bf16[64,3,2048]{2,1,0:T(4,128)(2,1)}), bf16[64,3,2048]{2,1,0:T(4,128)(2,1)}, u32[]{:S(2)}, u32[]{:S(2)}) %all-to-all-start.7) | async-done | bytes 786464 | tf_op jit(solution)/shard_map/all_to_all | solution.py:45
  298.6 20.2 %all-to-all-done.8 = bf16[64,3,2048]{2,1,0:T(4,128)(2,1)} async-done(((bf16[64,3,2048]{2,1,0:T(4,128)(2,1)}), bf16[64,3,2048]{2,1,0:T(4,128)(2,1)}, u32[]{:S(2)}, u32[]{:S(2)}) %all-to-all-start.8) | async-done | bytes 786464 | tf_op jit(solution)/shard_map/all_to_all | solution.py:52
  350.9 26.9 %all-to-all-done.10 = bf16[64,3,2048]{2,1,0:T(4,128)(2,1)} async-done(((bf16[64,3,2048]{2,1,0:T(4,128)(2,1)}), bf16[64,3,2048]{2,1,0:T(4,128)(2,1)}, u32[]{:S(2)}, u32[]{:S(2)}) %all-to-all-start.10) | async-done | bytes 786464 | tf_op jit(solution)/shard_map/all_to_all | solution.py:45
  399.7 21.5 %all-to-all-done.11 = bf16[64,3,2048]{2,1,0:T(4,128)(2,1)} async-done(((bf16[64,3,2048]{2,1,0:T(4,128)(2,1)}), bf16[64,3,2048]{2,1,0:T(4,128)(2,1)}, u32[]{:S(2)}, u32[]{:S(2)}) %all-to-all-start.11) | async-done | bytes 786464 | tf_op jit(solution)/shard_map/all_to_all | solution.py:52
  452.8 21.8 %all-to-all-done.13 = bf16[64,3,2048]{2,1,0:T(4,128)(2,1)} async-done(((bf16[64,3,2048]{2,1,0:T(4,128)(2,1)}), bf16[64,3,2048]{2,1,0:T(4,128)(2,1)}, u32[]{:S(2)}, u32[]{:S(2)}) %all-to-all-start.13) | async-done | bytes 786464 | tf_op jit(solution)/shard_map/all_to_all | solution.py:45
  486.5 24.1 %all-to-all-done.14 = bf16[64,3,2048]{2,1,0:T(4,128)(2,1)} async-done(((bf16[64,3,2048]{2,1,0:T(4,128)(2,1)}), bf16[64,3,2048]{2,1,0:T(4,128)(2,1)}, u32[]{:S(2)}, u32[]{:S(2)}) %all-to-all-start.14) | async-done | bytes 786464 | tf_op jit(solution)/shard_map/all_to_all | solution.py:52
  542.1 22.4 %all-to-all-done.16 = bf16[64,3,2048]{2,1,0:T(4,128)(2,1)} async-done(((bf16[64,3,2048]{2,1,0:T(4,128)(2,1)}), bf16[64,3,2048]{2,1,0:T(4,128)(2,1)}, u32[]{:S(2)}, u32[]{:S(2)}) %all-to-all-start.16) | async-done | bytes 786464 | tf_op jit(solution)/shard_map/all_to_all | solution.py:45
  580.6 26.7 %all-to-all-done.17 = bf16[64,3,2048]{2,1,0:T(4,128)(2,1)} async-done(((bf16[64,3,2048]{2,1,0:T(4,128)(2,1)}), bf16[64,3,2048]{2,1,0:T(4,128)(2,1)}, u32[]{:S(2)}, u32[]{:S(2)}) %all-to-all-start.17) | async-done | bytes 786464 | tf_op jit(solution)/shard_map/all_to_all | solution.py:52
  642.5 23.4 %all-to-all-done.19 = bf16[64,3,2048]{2,1,0:T(4,128)(2,1)} async-done(((bf16[64,3,2048]{2,1,0:T(4,128)(2,1)}), bf16[64,3,2048]{2,1,0:T(4,128)(2,1)}, u32[]{:S(2)}, u32[]{:S(2)}) %all-to-all-start.19) | async-done | bytes 786464 | tf_op jit(solution)/shard_map/all_to_all | solution.py:45
  701.7 20.6 %all-to-all-done.22 = bf16[64,3,2048]{2,1,0:T(4,128)(2,1)} async-done(((bf16[64,3,2048]{2,1,0:T(4,128)(2,1)}), bf16[64,3,2048]{2,1,0:T(4,128)(2,1)}, u32[]{:S(2)}, u32[]{:S(2)}) %all-to-all-start.22) | async-done | bytes 786464 | tf_op jit(solution)/shard_map/all_to_all | solution.py:60
  750.4 28.5 %all-to-all-done.23 = bf16[64,3,2048]{2,1,0:T(4,128)(2,1)} async-done(((bf16[64,3,2048]{2,1,0:T(4,128)(2,1)}), bf16[64,3,2048]{2,1,0:T(4,128)(2,1)}, u32[]{:S(2)}, u32[]{:S(2)}) %all-to-all-start.23) | async-done | bytes 786464 | tf_op jit(solution)/shard_map/all_to_all | solution.py:56
  788.4 19.0 %all-to-all-done.24 = bf16[64,3,2048]{2,1,0:T(4,128)(2,1)} async-done(((bf16[64,3,2048]{2,1,0:T(4,128)(2,1)}), bf16[64,3,2048]{2,1,0:T(4,128)(2,1)}, u32[]{:S(2)}, u32[]{:S(2)}) %all-to-all-start.24) | async-done | bytes 786464 | tf_op jit(solution)/shard_map/all_to_all | solution.py:60
  839.6 28.5 %all-to-all-done.25 = bf16[64,3,2048]{2,1,0:T(4,128)(2,1)} async-done(((bf16[64,3,2048]{2,1,0:T(4,128)(2,1)}), bf16[64,3,2048]{2,1,0:T(4,128)(2,1)}, u32[]{:S(2)}, u32[]{:S(2)}) %all-to-all-start.25) | async-done | bytes 786464 | tf_op jit(solution)/shard_map/all_to_all | solution.py:56
  877.8 19.0 %all-to-all-done.26 = bf16[64,3,2048]{2,1,0:T(4,128)(2,1)} async-done(((bf16[64,3,2048]{2,1,0:T(4,128)(2,1)}), bf16[64,3,2048]{2,1,0:T(4,128)(2,1)}, u32[]{:S(2)}, u32[]{:S(2)}) %all-to-all-start.26) | async-done | bytes 786464 | tf_op jit(solution)/shard_map/all_to_all | solution.py:60
  902.2 17.1 %collective-permute-done.8 = bf16[32,2048]{1,0:T(8,128)(2,1)S(1)} collective-permute-done((bf16[32,2048]{1,0:T(8,128)(2,1)S(1)}, bf16[32,2048]{1,0:T(8,128)(2,1)S(1)}, u32[]{:S(2)}, u32[]{:S(2)}) %collective-permute-start.8) | collective-permute-done | bytes 131104 | tf_op jit(solution)/shard_map/ppermute | solution.py:13
  930.2 28.5 %all-to-all-done.27 = bf16[64,3,2048]{2,1,0:T(4,128)(2,1)} async-done(((bf16[64,3,2048]{2,1,0:T(4,128)(2,1)}), bf16[64,3,2048]{2,1,0:T(4,128)(2,1)}, u32[]{:S(2)}, u32[]{:S(2)}) %all-to-all-start.27) | async-done | bytes 786464 | tf_op jit(solution)/shard_map/all_to_all | solution.py:56
  976.9 19.1 %all-to-all-done.28 = bf16[64,3,2048]{2,1,0:T(4,128)(2,1)} async-done(((bf16[64,3,2048]{2,1,0:T(4,128)(2,1)}), bf16[64,3,2048]{2,1,0:T(4,128)(2,1)}, u32[]{:S(2)}, u32[]{:S(2)}) %all-to-all-start.28) | async-done | bytes 786464 | tf_op jit(solution)/shard_map/all_to_all | solution.py:60
  1020.2 28.5 %all-to-all-done.29 = bf16[64,3,2048]{2,1,0:T(4,128)(2,1)} async-done(((bf16[64,3,2048]{2,1,0:T(4,128)(2,1)}), bf16[64,3,2048]{2,1,0:T(4,128)(2,1)}, u32[]{:S(2)}, u32[]{:S(2)}) %all-to-all-start.29) | async-done | bytes 786464 | tf_op jit(solution)/shard_map/all_to_all | solution.py:56
  1066.9 19.1 %all-to-all-done.30 = bf16[64,3,2048]{2,1,0:T(4,128)(2,1)} async-done(((bf16[64,3,2048]{2,1,0:T(4,128)(2,1)}), bf16[64,3,2048]{2,1,0:T(4,128)(2,1)}, u32[]{:S(2)}, u32[]{:S(2)}) %all-to-all-start.30) | async-done | bytes 786464 | tf_op jit(solution)/shard_map/all_to_all | solution.py:60
  1091.4 23.4 %collective-permute-done.10 = bf16[32,2048]{1,0:T(8,128)(2,1)S(1)} collective-permute-done((bf16[32,2048]{1,0:T(8,128)(2,1)S(1)}, bf16[32,2048]{1,0:T(8,128)(2,1)S(1)}, u32[]{:S(2)}, u32[]{:S(2)}) %collective-permute-start.10) | collective-permute-done | bytes 131104 | tf_op jit(solution)/shard_map/ppermute | solution.py:13
  1123.6 28.0 %all-to-all-done.31 = bf16[64,3,2048]{2,1,0:T(4,128)(2,1)} async-done(((bf16[64,3,2048]{2,1,0:T(4,128)(2,1)}), bf16[64,3,2048]{2,1,0:T(4,128)(2,1)}, u32[]{:S(2)}, u32[]{:S(2)}) %all-to-all-start.31) | async-done | bytes 786464 | tf_op jit(solution)/shard_map/all_to_all | solution.py:56
  1170.2 27.8 %all-to-all-done.32 = bf16[64,3,2048]{2,1,0:T(4,128)(2,1)} async-done(((bf16[64,3,2048]{2,1,0:T(4,128)(2,1)}), bf16[64,3,2048]{2,1,0:T(4,128)(2,1)}, u32[]{:S(2)}, u32[]{:S(2)}) %all-to-all-start.32) | async-done | bytes 786464 | tf_op jit(solution)/shard_map/all_to_all | solution.py:60
  1224.8 18.5 %all-to-all-done.33 = bf16[64,3,2048]{2,1,0:T(4,128)(2,1)} async-done(((bf16[64,3,2048]{2,1,0:T(4,128)(2,1)}), bf16[64,3,2048]{2,1,0:T(4,128)(2,1)}, u32[]{:S(2)}, u32[]{:S(2)}) %all-to-all-start.33) | async-done | bytes 786464 | tf_op jit(solution)/shard_map/all_to_all | solution.py:56
  1281.5 18.8 %all-to-all-done.34 = bf16[64,3,2048]{2,1,0:T(4,128)(2,1)S(1)} async-done(((bf16[64,3,2048]{2,1,0:T(4,128)(2,1)}), bf16[64,3,2048]{2,1,0:T(4,128)(2,1)S(1)}, u32[]{:S(2)}, u32[]{:S(2)}) %all-to-all-start.34) | async-done | bytes 786464 | tf_op jit(solution)/shard_map/all_to_all | solution.py:60
  1302.3 203.1 %psum.7 = f32[1,2048]{1,0:T(1,128)} all-reduce(f32[1,2048]{1,0:T(1,128)S(1)} %bitcast.633), channel_id=1, replica_groups=mesh['dp'=8,'pipe'=4,'expert'=8] {'dp','expert'}, use_global_device_ids=true, to_apply=%region_84.85 | all-reduce | flops 2048 | bytes 16384 | tf_op jit(solution)/shard_map/psum | solution.py:226
  (408 shorter events, 687.5 us)
Async XLA Ops:
  5.5 27.2 %all-to-all-start = ((bf16[64,3,1]{1,2,0:T(2,128)(2,1)}), bf16[64,3,1]{1,2,0:T(2,128)(2,1)S(1)}, u32[]{:S(2)}, u32[]{:S(2)}) async-start(bf16[64,3,1]{1,2,0:T(2,128)(2,1)} %copy.214), calls=%async_computation | async-start | bytes 65536 | tf_op jit(solution)/shard_map/all_to_all | solution.py:46
  32.7 33.2 %all-to-all-start.1 = ((bf16[64,3,2048]{2,1,0:T(4,128)(2,1)}), bf16[64,3,2048]{2,1,0:T(4,128)(2,1)}, u32[]{:S(2)}, u32[]{:S(2)}) async-start(bf16[64,3,2048]{2,1,0:T(4,128)(2,1)} %copy.215), calls=%async_computation.1 | async-start | bytes 2097152 | tf_op jit(solution)/shard_map/all_to_all | solution.py:45
  78.3 24.5 %all-to-all-start.2 = ((bf16[64,3,2048]{2,1,0:T(4,128)(2,1)}), bf16[64,3,2048]{2,1,0:T(4,128)(2,1)}, u32[]{:S(2)}, u32[]{:S(2)}) async-start(bf16[64,3,2048]{2,1,0:T(4,128)(2,1)} %reshape.639), calls=%async_computation.2 | async-start | bytes 2097152 | tf_op jit(solution)/shard_map/all_to_all | solution.py:52
  122.4 43.0 %all-to-all-start.4 = ((bf16[64,3,2048]{2,1,0:T(4,128)(2,1)}), bf16[64,3,2048]{2,1,0:T(4,128)(2,1)}, u32[]{:S(2)}, u32[]{:S(2)}) async-start(bf16[64,3,2048]{2,1,0:T(4,128)(2,1)} %copy.219), calls=%async_computation.4 | async-start | bytes 2097152 | tf_op jit(solution)/shard_map/all_to_all | solution.py:45
  178.0 24.5 %all-to-all-start.5 = ((bf16[64,3,2048]{2,1,0:T(4,128)(2,1)}), bf16[64,3,2048]{2,1,0:T(4,128)(2,1)}, u32[]{:S(2)}, u32[]{:S(2)}) async-start(bf16[64,3,2048]{2,1,0:T(4,128)(2,1)} %reshape.641), calls=%async_computation.5 | async-start | bytes 2097152 | tf_op jit(solution)/shard_map/all_to_all | solution.py:52
  205.4 23.7 %collective-permute-start.1 = (bf16[32,2048]{1,0:T(8,128)(2,1)S(1)}, bf16[32,2048]{1,0:T(8,128)(2,1)S(1)}, u32[]{:S(2)}, u32[]{:S(2)}) collective-permute-start(bf16[32,2048]{1,0:T(8,128)(2,1)S(1)} %get-tuple-element.841), channel_id=1, source_target_pairs={{0,8},{8,16},{16,24},{1,9},{9,17},{17,25},{2,10},{10,18},{18,26},{... | collective-permute-start | bytes 393224 | tf_op jit(solution)/shard_map/ppermute | solution.py:13
  240.8 34.5 %all-to-all-start.7 = ((bf16[64,3,2048]{2,1,0:T(4,128)(2,1)}), bf16[64,3,2048]{2,1,0:T(4,128)(2,1)}, u32[]{:S(2)}, u32[]{:S(2)}) async-start(bf16[64,3,2048]{2,1,0:T(4,128)(2,1)} %copy.223), calls=%async_computation.7 | async-start | bytes 2097152 | tf_op jit(solution)/shard_map/all_to_all | solution.py:45
  287.7 31.1 %all-to-all-start.8 = ((bf16[64,3,2048]{2,1,0:T(4,128)(2,1)}), bf16[64,3,2048]{2,1,0:T(4,128)(2,1)}, u32[]{:S(2)}, u32[]{:S(2)}) async-start(bf16[64,3,2048]{2,1,0:T(4,128)(2,1)} %reshape.643), calls=%async_computation.8 | async-start | bytes 2097152 | tf_op jit(solution)/shard_map/all_to_all | solution.py:52
  324.2 20.9 %all-to-all-start.9 = ((bf16[64,3,1]{1,2,0:T(2,128)(2,1)}), bf16[64,3,1]{1,2,0:T(2,128)(2,1)S(1)}, u32[]{:S(2)}, u32[]{:S(2)}) async-start(bf16[64,3,1]{1,2,0:T(2,128)(2,1)} %copy.226), calls=%async_computation.9 | async-start | bytes 65536 | tf_op jit(solution)/shard_map/all_to_all | solution.py:46
  345.1 32.7 %all-to-all-start.10 = ((bf16[64,3,2048]{2,1,0:T(4,128)(2,1)}), bf16[64,3,2048]{2,1,0:T(4,128)(2,1)}, u32[]{:S(2)}, u32[]{:S(2)}) async-start(bf16[64,3,2048]{2,1,0:T(4,128)(2,1)} %copy.227), calls=%async_computation.10 | async-start | bytes 2097152 | tf_op jit(solution)/shard_map/all_to_all | solution.py:45
  390.2 31.1 %all-to-all-start.11 = ((bf16[64,3,2048]{2,1,0:T(4,128)(2,1)}), bf16[64,3,2048]{2,1,0:T(4,128)(2,1)}, u32[]{:S(2)}, u32[]{:S(2)}) async-start(bf16[64,3,2048]{2,1,0:T(4,128)(2,1)} %reshape.645), calls=%async_computation.11 | async-start | bytes 2097152 | tf_op jit(solution)/shard_map/all_to_all | solution.py:52
  447.0 27.6 %all-to-all-start.13 = ((bf16[64,3,2048]{2,1,0:T(4,128)(2,1)}), bf16[64,3,2048]{2,1,0:T(4,128)(2,1)}, u32[]{:S(2)}, u32[]{:S(2)}) async-start(bf16[64,3,2048]{2,1,0:T(4,128)(2,1)} %copy.231), calls=%async_computation.13 | async-start | bytes 2097152 | tf_op jit(solution)/shard_map/all_to_all | solution.py:45
  479.9 30.7 %all-to-all-start.14 = ((bf16[64,3,2048]{2,1,0:T(4,128)(2,1)}), bf16[64,3,2048]{2,1,0:T(4,128)(2,1)}, u32[]{:S(2)}, u32[]{:S(2)}) async-start(bf16[64,3,2048]{2,1,0:T(4,128)(2,1)} %reshape.647), calls=%async_computation.14 | async-start | bytes 2097152 | tf_op jit(solution)/shard_map/all_to_all | solution.py:52
  536.3 28.2 %all-to-all-start.16 = ((bf16[64,3,2048]{2,1,0:T(4,128)(2,1)}), bf16[64,3,2048]{2,1,0:T(4,128)(2,1)}, u32[]{:S(2)}, u32[]{:S(2)}) async-start(bf16[64,3,2048]{2,1,0:T(4,128)(2,1)} %copy.235), calls=%async_computation.16 | async-start | bytes 2097152 | tf_op jit(solution)/shard_map/all_to_all | solution.py:45
  569.6 37.7 %all-to-all-start.17 = ((bf16[64,3,2048]{2,1,0:T(4,128)(2,1)}), bf16[64,3,2048]{2,1,0:T(4,128)(2,1)}, u32[]{:S(2)}, u32[]{:S(2)}) async-start(bf16[64,3,2048]{2,1,0:T(4,128)(2,1)} %reshape.649), calls=%async_computation.17 | async-start | bytes 2097152 | tf_op jit(solution)/shard_map/all_to_all | solution.py:52
  631.6 34.4 %all-to-all-start.19 = ((bf16[64,3,2048]{2,1,0:T(4,128)(2,1)}), bf16[64,3,2048]{2,1,0:T(4,128)(2,1)}, u32[]{:S(2)}, u32[]{:S(2)}) async-start(bf16[64,3,2048]{2,1,0:T(4,128)(2,1)} %copy.239), calls=%async_computation.19 | async-start | bytes 2097152 | tf_op jit(solution)/shard_map/all_to_all | solution.py:45
  666.0 24.4 %all-to-all-start.21 = ((bf16[64,3,2048]{2,1,0:T(4,128)(2,1)}), bf16[64,3,2048]{2,1,0:T(4,128)(2,1)}, u32[]{:S(2)}, u32[]{:S(2)}) async-start(bf16[64,3,2048]{2,1,0:T(4,128)(2,1)} %copy.242), calls=%async_computation.21 | async-start | bytes 2097152 | tf_op jit(solution)/shard_map/all_to_all | solution.py:56
  694.6 27.6 %all-to-all-start.22 = ((bf16[64,3,2048]{2,1,0:T(4,128)(2,1)}), bf16[64,3,2048]{2,1,0:T(4,128)(2,1)}, u32[]{:S(2)}, u32[]{:S(2)}) async-start(bf16[64,3,2048]{2,1,0:T(4,128)(2,1)} %reshape.654), calls=%async_computation.22 | async-start | bytes 2097152 | tf_op jit(solution)/shard_map/all_to_all | solution.py:60
  744.6 34.2 %all-to-all-start.23 = ((bf16[64,3,2048]{2,1,0:T(4,128)(2,1)}), bf16[64,3,2048]{2,1,0:T(4,128)(2,1)}, u32[]{:S(2)}, u32[]{:S(2)}) async-start(bf16[64,3,2048]{2,1,0:T(4,128)(2,1)} %copy.251), calls=%async_computation.23 | async-start | bytes 2097152 | tf_op jit(solution)/shard_map/all_to_all | solution.py:56
  783.1 24.3 %all-to-all-start.24 = ((bf16[64,3,2048]{2,1,0:T(4,128)(2,1)}), bf16[64,3,2048]{2,1,0:T(4,128)(2,1)}, u32[]{:S(2)}, u32[]{:S(2)}) async-start(bf16[64,3,2048]{2,1,0:T(4,128)(2,1)} %reshape.656), calls=%async_computation.24 | async-start | bytes 2097152 | tf_op jit(solution)/shard_map/all_to_all | solution.py:60
  827.4 40.7 %all-to-all-start.25 = ((bf16[64,3,2048]{2,1,0:T(4,128)(2,1)}), bf16[64,3,2048]{2,1,0:T(4,128)(2,1)}, u32[]{:S(2)}, u32[]{:S(2)}) async-start(bf16[64,3,2048]{2,1,0:T(4,128)(2,1)} %copy.253), calls=%async_computation.25 | async-start | bytes 2097152 | tf_op jit(solution)/shard_map/all_to_all | solution.py:56
  872.5 24.3 %all-to-all-start.26 = ((bf16[64,3,2048]{2,1,0:T(4,128)(2,1)}), bf16[64,3,2048]{2,1,0:T(4,128)(2,1)}, u32[]{:S(2)}, u32[]{:S(2)}) async-start(bf16[64,3,2048]{2,1,0:T(4,128)(2,1)} %reshape.658), calls=%async_computation.26 | async-start | bytes 2097152 | tf_op jit(solution)/shard_map/all_to_all | solution.py:60
  922.4 36.3 %all-to-all-start.27 = ((bf16[64,3,2048]{2,1,0:T(4,128)(2,1)}), bf16[64,3,2048]{2,1,0:T(4,128)(2,1)}, u32[]{:S(2)}, u32[]{:S(2)}) async-start(bf16[64,3,2048]{2,1,0:T(4,128)(2,1)} %copy.255), calls=%async_computation.27 | async-start | bytes 2097152 | tf_op jit(solution)/shard_map/all_to_all | solution.py:56
  971.6 24.4 %all-to-all-start.28 = ((bf16[64,3,2048]{2,1,0:T(4,128)(2,1)}), bf16[64,3,2048]{2,1,0:T(4,128)(2,1)}, u32[]{:S(2)}, u32[]{:S(2)}) async-start(bf16[64,3,2048]{2,1,0:T(4,128)(2,1)} %reshape.660), calls=%async_computation.28 | async-start | bytes 2097152 | tf_op jit(solution)/shard_map/all_to_all | solution.py:60
  1012.4 36.3 %all-to-all-start.29 = ((bf16[64,3,2048]{2,1,0:T(4,128)(2,1)}), bf16[64,3,2048]{2,1,0:T(4,128)(2,1)}, u32[]{:S(2)}, u32[]{:S(2)}) async-start(bf16[64,3,2048]{2,1,0:T(4,128)(2,1)} %copy.257), calls=%async_computation.29 | async-start | bytes 2097152 | tf_op jit(solution)/shard_map/all_to_all | solution.py:56
  1061.6 24.4 %all-to-all-start.30 = ((bf16[64,3,2048]{2,1,0:T(4,128)(2,1)}), bf16[64,3,2048]{2,1,0:T(4,128)(2,1)}, u32[]{:S(2)}, u32[]{:S(2)}) async-start(bf16[64,3,2048]{2,1,0:T(4,128)(2,1)} %reshape.662), calls=%async_computation.30 | async-start | bytes 2097152 | tf_op jit(solution)/shard_map/all_to_all | solution.py:60
  1090.1 24.7 %collective-permute-start.10 = (bf16[32,2048]{1,0:T(8,128)(2,1)S(1)}, bf16[32,2048]{1,0:T(8,128)(2,1)S(1)}, u32[]{:S(2)}, u32[]{:S(2)}) collective-permute-start(bf16[32,2048]{1,0:T(8,128)(2,1)S(1)} %get-tuple-element.782), channel_id=1, source_target_pairs={{8,0},{16,8},{24,16},{9,1},{17,9},{25,17},{10,2},{18,10},{26,18},{... | collective-permute-start | bytes 393224 | tf_op jit(solution)/shard_map/ppermute | solution.py:13
  1117.9 33.7 %all-to-all-start.31 = ((bf16[64,3,2048]{2,1,0:T(4,128)(2,1)}), bf16[64,3,2048]{2,1,0:T(4,128)(2,1)}, u32[]{:S(2)}, u32[]{:S(2)}) async-start(bf16[64,3,2048]{2,1,0:T(4,128)(2,1)} %copy.259), calls=%async_computation.31 | async-start | bytes 2097152 | tf_op jit(solution)/shard_map/all_to_all | solution.py:56
  1164.6 33.5 %all-to-all-start.32 = ((bf16[64,3,2048]{2,1,0:T(4,128)(2,1)}), bf16[64,3,2048]{2,1,0:T(4,128)(2,1)}, u32[]{:S(2)}, u32[]{:S(2)}) async-start(bf16[64,3,2048]{2,1,0:T(4,128)(2,1)} %reshape.664), calls=%async_computation.32 | async-start | bytes 2097152 | tf_op jit(solution)/shard_map/all_to_all | solution.py:60
  1211.5 31.9 %all-to-all-start.33 = ((bf16[64,3,2048]{2,1,0:T(4,128)(2,1)}), bf16[64,3,2048]{2,1,0:T(4,128)(2,1)}, u32[]{:S(2)}, u32[]{:S(2)}) async-start(bf16[64,3,2048]{2,1,0:T(4,128)(2,1)} %copy.261), calls=%async_computation.33 | async-start | bytes 2097152 | tf_op jit(solution)/shard_map/all_to_all | solution.py:56
  1243.3 29.7 %all-to-all-start.20 = ((bf16[64,3,2048]{2,1,0:T(4,128)(2,1)}), bf16[64,3,2048]{2,1,0:T(4,128)(2,1)}, u32[]{:S(2)}, u32[]{:S(2)}) async-start(bf16[64,3,2048]{2,1,0:T(4,128)(2,1)} %reshape.651), calls=%async_computation.20 | async-start | bytes 2097152 | tf_op jit(solution)/shard_map/all_to_all | solution.py:52
  1273.1 27.2 %all-to-all-start.34 = ((bf16[64,3,2048]{2,1,0:T(4,128)(2,1)}), bf16[64,3,2048]{2,1,0:T(4,128)(2,1)S(1)}, u32[]{:S(2)}, u32[]{:S(2)}) async-start(bf16[64,3,2048]{2,1,0:T(4,128)(2,1)} %reshape.666), calls=%async_computation.34 | async-start | bytes 2097152 | tf_op jit(solution)/shard_map/all_to_all | solution.py:60
  (43 other events, 645.2 us)
where the time goes:
time: 1520 us; the launch traced here: 1510 us
  waiting for transfers between devices  747 us (49%)
  starting transfers between devices  290 us (19%)
  blocking collectives  203 us (13%)
  local copies, waits for them, and re-layouts  141 us (9%)
  matrix products  92.5 us (6%)
  other arithmetic  31.6 us (2%)
    psum x1, blocking collectives, body(): gain_grad = lax.psum(gain_sum, ('dp', 'expert'))  203 us
    all_to_all x7, waiting for transfers between devices, send_rows(): lax.all_to_all(row_block, ('dp', 'expert'), split_axis=0, concat_axis=0,...  177 us
    all_to_all x7, waiting for transfers between devices, send_grads(): lax.all_to_all(row_block, ('dp', 'expert'), split_axis=0, concat_axis=0,...  165 us
    all_to_all x7, waiting for transfers between devices, return_grads(): lax.all_to_all(row_block, ('dp', 'expert'), split_axis=0, concat_axis=0,...  144 us
    all_to_all x7, waiting for transfers between devices, return_rows(): lax.all_to_all(row_block, ('dp', 'expert'), split_axis=0, concat_axis=0,...  138 us
    ppermute x12, waiting for transfers between devices, from_behind(): lax.ppermute(value, axis, [(source, source + steps) for source in range(l...  79.9 us
    all_to_all x7, starting transfers between devices, send_rows(): lax.all_to_all(pair_block, ('dp', 'expert'), split_axis=0, concat_axis=0,...  58 us
    all_to_all x7, starting transfers between devices, send_grads(): lax.all_to_all(row_block, ('dp', 'expert'), split_axis=0, concat_axis=0,...  54.3 us
  transfers between devices with their start and end apart: 47, of which 41 were waited for; matrix products, arithmetic and copies ran while one was open for 5% of the time, Pallas kernels for 0%

commit v1 on v0

--- a/solution.py
+++ b/solution.py
@@ -223,7 +223,9 @@
         gain_sum = gain_sum + gain_term
         if tick_num + 1 < ticks:
             incoming = from_behind(grad_bf, "pipe", -1)
-    gain_grad = lax.psum(gain_sum, ("dp", "expert"))
+    gain_grad = gain_sum
+    for tick in ("expert", "dp"):
+        gain_grad = lax.psum(gain_grad, tick)
     segment_out = layer_outs[:MICRO].reshape(1, tok_rows, width)
     segment_grad = grad_outs[:MICRO].reshape(1, tok_rows, width)
     return (segment_out, segment_grad, gain_grad.reshape(1, width))

time: 1520 us -> 1360 us (0.89)
  blocking collectives: 203 us -> 35 us
    psum x1 -> x2, blocking collectives: 203 us -> 35 us  [body(): gain_grad = lax.psum(gain_grad, tick)]
  transfers between devices with their start and end apart: 47 -> 47, of which waited for: 41 -> 41; matrix products, arithmetic and copies ran while one was open for 5% -> 6% of each run, Pallas kernels for 0% -> 0%
where the time goes in v1:
time: 1360 us; the launch traced here: 1340 us
  waiting for transfers between devices  747 us (55%)
  starting transfers between devices  290 us (21%)
  local copies, waits for them, and re-layouts  141 us (10%)
  matrix products  92.5 us (7%)
  blocking collectives  35 us (3%)
  other arithmetic  31.6 us (2%)
    all_to_all x7, waiting for transfers between devices, send_rows(): lax.all_to_all(row_block, ('dp', 'expert'), split_axis=0, concat_axis=0,...  177 us
    all_to_all x7, waiting for transfers between devices, send_grads(): lax.all_to_all(row_block, ('dp', 'expert'), split_axis=0, concat_axis=0,...  165 us
    all_to_all x7, waiting for transfers between devices, return_grads(): lax.all_to_all(row_block, ('dp', 'expert'), split_axis=0, concat_axis=0,...  143 us
    all_to_all x7, waiting for transfers between devices, return_rows(): lax.all_to_all(row_block, ('dp', 'expert'), split_axis=0, concat_axis=0,...  138 us
    ppermute x12, waiting for transfers between devices, from_behind(): lax.ppermute(value, axis, [(source, source + steps) for source in range(l...  79.9 us
    all_to_all x7, starting transfers between devices, send_rows(): lax.all_to_all(pair_block, ('dp', 'expert'), split_axis=0, concat_axis=0,...  58 us
    all_to_all x7, starting transfers between devices, send_grads(): lax.all_to_all(row_block, ('dp', 'expert'), split_axis=0, concat_axis=0,...  54.3 us
    all_to_all x7, starting transfers between devices, return_rows(): lax.all_to_all(row_block, ('dp', 'expert'), split_axis=0, concat_axis=0,...  50.9 us
  transfers between devices with their start and end apart: 47, of which 41 were waited for; matrix products, arithmetic and copies ran while one was open for 6% of the time, Pallas kernels for 0%

profile of v1, /device:TPU:1, one launch (start us, length us, event | category | flops | bytes accessed | tf_op | source)
XLA Modules:
  0.0 1339.5 jit_solution(3824412371757008780)
XLA Ops:
  5.5 15.6 %all-to-all-start = ((bf16[64,3,1]{1,2,0:T(2,128)(2,1)}), bf16[64,3,1]{1,2,0:T(2,128)(2,1)S(1)}, u32[]{:S(2)}, u32[]{:S(2)}) async-start(bf16[64,3,1]{1,2,0:T(2,128)(2,1)} %copy.214), calls=%async_computation | async-start | bytes 65536 | tf_op jit(solution)/shard_map/all_to_all | solution.py:46
  40.4 25.5 %all-to-all-done.1 = bf16[64,3,2048]{2,1,0:T(4,128)(2,1)} async-done(((bf16[64,3,2048]{2,1,0:T(4,128)(2,1)}), bf16[64,3,2048]{2,1,0:T(4,128)(2,1)}, u32[]{:S(2)}, u32[]{:S(2)}) %all-to-all-start.1) | async-done | bytes 786464 | tf_op jit(solution)/shard_map/all_to_all | solution.py:45
  84.8 18.1 %all-to-all-done.2 = bf16[64,3,2048]{2,1,0:T(4,128)(2,1)} async-done(((bf16[64,3,2048]{2,1,0:T(4,128)(2,1)}), bf16[64,3,2048]{2,1,0:T(4,128)(2,1)}, u32[]{:S(2)}, u32[]{:S(2)}) %all-to-all-start.2) | async-done | bytes 786464 | tf_op jit(solution)/shard_map/all_to_all | solution.py:52
  122.4 14.5 %all-to-all-start.4 = ((bf16[64,3,2048]{2,1,0:T(4,128)(2,1)}), bf16[64,3,2048]{2,1,0:T(4,128)(2,1)}, u32[]{:S(2)}, u32[]{:S(2)}) async-start(bf16[64,3,2048]{2,1,0:T(4,128)(2,1)} %copy.219), calls=%async_computation.4 | async-start | bytes 2097152 | tf_op jit(solution)/shard_map/all_to_all | solution.py:45
  136.9 28.5 %all-to-all-done.4 = bf16[64,3,2048]{2,1,0:T(4,128)(2,1)} async-done(((bf16[64,3,2048]{2,1,0:T(4,128)(2,1)}), bf16[64,3,2048]{2,1,0:T(4,128)(2,1)}, u32[]{:S(2)}, u32[]{:S(2)}) %all-to-all-start.4) | async-done | bytes 786464 | tf_op jit(solution)/shard_map/all_to_all | solution.py:45
  184.1 18.4 %all-to-all-done.5 = bf16[64,3,2048]{2,1,0:T(4,128)(2,1)} async-done(((bf16[64,3,2048]{2,1,0:T(4,128)(2,1)}), bf16[64,3,2048]{2,1,0:T(4,128)(2,1)}, u32[]{:S(2)}, u32[]{:S(2)}) %all-to-all-start.5) | async-done | bytes 786464 | tf_op jit(solution)/shard_map/all_to_all | solution.py:52
  205.4 17.4 %collective-permute-start.1 = (bf16[32,2048]{1,0:T(8,128)(2,1)S(1)}, bf16[32,2048]{1,0:T(8,128)(2,1)S(1)}, u32[]{:S(2)}, u32[]{:S(2)}) collective-permute-start(bf16[32,2048]{1,0:T(8,128)(2,1)S(1)} %get-tuple-element.841), channel_id=1, source_target_pairs={{0,8},{8,16},{16,24},{1,9},{9,17},{17,25},{2,10},{10,18},{18,26},{... | collective-permute-start | bytes 393224 | tf_op jit(solution)/shard_map/ppermute | solution.py:13
  246.7 28.6 %all-to-all-done.7 = bf16[64,3,2048]{2,1,0:T(4,128)(2,1)} async-done(((bf16[64,3,2048]{2,1,0:T(4,128)(2,1)}), bf16[64,3,2048]{2,1,0:T(4,128)(2,1)}, u32[]{:S(2)}, u32[]{:S(2)}) %all-to-all-start.7) | async-done | bytes 786464 | tf_op jit(solution)/shard_map/all_to_all | solution.py:45
  298.6 20.2 %all-to-all-done.8 = bf16[64,3,2048]{2,1,0:T(4,128)(2,1)} async-done(((bf16[64,3,2048]{2,1,0:T(4,128)(2,1)}), bf16[64,3,2048]{2,1,0:T(4,128)(2,1)}, u32[]{:S(2)}, u32[]{:S(2)}) %all-to-all-start.8) | async-done | bytes 786464 | tf_op jit(solution)/shard_map/all_to_all | solution.py:52
  350.9 26.9 %all-to-all-done.10 = bf16[64,3,2048]{2,1,0:T(4,128)(2,1)} async-done(((bf16[64,3,2048]{2,1,0:T(4,128)(2,1)}), bf16[64,3,2048]{2,1,0:T(4,128)(2,1)}, u32[]{:S(2)}, u32[]{:S(2)}) %all-to-all-start.10) | async-done | bytes 786464 | tf_op jit(solution)/shard_map/all_to_all | solution.py:45
  399.7 21.5 %all-to-all-done.11 = bf16[64,3,2048]{2,1,0:T(4,128)(2,1)} async-done(((bf16[64,3,2048]{2,1,0:T(4,128)(2,1)}), bf16[64,3,2048]{2,1,0:T(4,128)(2,1)}, u32[]{:S(2)}, u32[]{:S(2)}) %all-to-all-start.11) | async-done | bytes 786464 | tf_op jit(solution)/shard_map/all_to_all | solution.py:52
  452.8 21.8 %all-to-all-done.13 = bf16[64,3,2048]{2,1,0:T(4,128)(2,1)} async-done(((bf16[64,3,2048]{2,1,0:T(4,128)(2,1)}), bf16[64,3,2048]{2,1,0:T(4,128)(2,1)}, u32[]{:S(2)}, u32[]{:S(2)}) %all-to-all-start.13) | async-done | bytes 786464 | tf_op jit(solution)/shard_map/all_to_all | solution.py:45
  486.5 24.1 %all-to-all-done.14 = bf16[64,3,2048]{2,1,0:T(4,128)(2,1)} async-done(((bf16[64,3,2048]{2,1,0:T(4,128)(2,1)}), bf16[64,3,2048]{2,1,0:T(4,128)(2,1)}, u32[]{:S(2)}, u32[]{:S(2)}) %all-to-all-start.14) | async-done | bytes 786464 | tf_op jit(solution)/shard_map/all_to_all | solution.py:52
  542.1 22.4 %all-to-all-done.16 = bf16[64,3,2048]{2,1,0:T(4,128)(2,1)} async-done(((bf16[64,3,2048]{2,1,0:T(4,128)(2,1)}), bf16[64,3,2048]{2,1,0:T(4,128)(2,1)}, u32[]{:S(2)}, u32[]{:S(2)}) %all-to-all-start.16) | async-done | bytes 786464 | tf_op jit(solution)/shard_map/all_to_all | solution.py:45
  580.6 26.7 %all-to-all-done.17 = bf16[64,3,2048]{2,1,0:T(4,128)(2,1)} async-done(((bf16[64,3,2048]{2,1,0:T(4,128)(2,1)}), bf16[64,3,2048]{2,1,0:T(4,128)(2,1)}, u32[]{:S(2)}, u32[]{:S(2)}) %all-to-all-start.17) | async-done | bytes 786464 | tf_op jit(solution)/shard_map/all_to_all | solution.py:52
  642.5 23.4 %all-to-all-done.19 = bf16[64,3,2048]{2,1,0:T(4,128)(2,1)} async-done(((bf16[64,3,2048]{2,1,0:T(4,128)(2,1)}), bf16[64,3,2048]{2,1,0:T(4,128)(2,1)}, u32[]{:S(2)}, u32[]{:S(2)}) %all-to-all-start.19) | async-done | bytes 786464 | tf_op jit(solution)/shard_map/all_to_all | solution.py:45
  701.7 20.6 %all-to-all-done.22 = bf16[64,3,2048]{2,1,0:T(4,128)(2,1)} async-done(((bf16[64,3,2048]{2,1,0:T(4,128)(2,1)}), bf16[64,3,2048]{2,1,0:T(4,128)(2,1)}, u32[]{:S(2)}, u32[]{:S(2)}) %all-to-all-start.22) | async-done | bytes 786464 | tf_op jit(solution)/shard_map/all_to_all | solution.py:60
  750.4 28.5 %all-to-all-done.23 = bf16[64,3,2048]{2,1,0:T(4,128)(2,1)} async-done(((bf16[64,3,2048]{2,1,0:T(4,128)(2,1)}), bf16[64,3,2048]{2,1,0:T(4,128)(2,1)}, u32[]{:S(2)}, u32[]{:S(2)}) %all-to-all-start.23) | async-done | bytes 786464 | tf_op jit(solution)/shard_map/all_to_all | solution.py:56
  788.4 19.0 %all-to-all-done.24 = bf16[64,3,2048]{2,1,0:T(4,128)(2,1)} async-done(((bf16[64,3,2048]{2,1,0:T(4,128)(2,1)}), bf16[64,3,2048]{2,1,0:T(4,128)(2,1)}, u32[]{:S(2)}, u32[]{:S(2)}) %all-to-all-start.24) | async-done | bytes 786464 | tf_op jit(solution)/shard_map/all_to_all | solution.py:60
  839.6 28.5 %all-to-all-done.25 = bf16[64,3,2048]{2,1,0:T(4,128)(2,1)} async-done(((bf16[64,3,2048]{2,1,0:T(4,128)(2,1)}), bf16[64,3,2048]{2,1,0:T(4,128)(2,1)}, u32[]{:S(2)}, u32[]{:S(2)}) %all-to-all-start.25) | async-done | bytes 786464 | tf_op jit(solution)/shard_map/all_to_all | solution.py:56
  877.8 19.0 %all-to-all-done.26 = bf16[64,3,2048]{2,1,0:T(4,128)(2,1)} async-done(((bf16[64,3,2048]{2,1,0:T(4,128)(2,1)}), bf16[64,3,2048]{2,1,0:T(4,128)(2,1)}, u32[]{:S(2)}, u32[]{:S(2)}) %all-to-all-start.26) | async-done | bytes 786464 | tf_op jit(solution)/shard_map/all_to_all | solution.py:60
  902.2 17.1 %collective-permute-done.8 = bf16[32,2048]{1,0:T(8,128)(2,1)S(1)} collective-permute-done((bf16[32,2048]{1,0:T(8,128)(2,1)S(1)}, bf16[32,2048]{1,0:T(8,128)(2,1)S(1)}, u32[]{:S(2)}, u32[]{:S(2)}) %collective-permute-start.8) | collective-permute-done | bytes 131104 | tf_op jit(solution)/shard_map/ppermute | solution.py:13
  930.2 28.5 %all-to-all-done.27 = bf16[64,3,2048]{2,1,0:T(4,128)(2,1)} async-done(((bf16[64,3,2048]{2,1,0:T(4,128)(2,1)}), bf16[64,3,2048]{2,1,0:T(4,128)(2,1)}, u32[]{:S(2)}, u32[]{:S(2)}) %all-to-all-start.27) | async-done | bytes 786464 | tf_op jit(solution)/shard_map/all_to_all | solution.py:56
  976.9 19.1 %all-to-all-done.28 = bf16[64,3,2048]{2,1,0:T(4,128)(2,1)} async-done(((bf16[64,3,2048]{2,1,0:T(4,128)(2,1)}), bf16[64,3,2048]{2,1,0:T(4,128)(2,1)}, u32[]{:S(2)}, u32[]{:S(2)}) %all-to-all-start.28) | async-done | bytes 786464 | tf_op jit(solution)/shard_map/all_to_all | solution.py:60
  1020.2 28.5 %all-to-all-done.29 = bf16[64,3,2048]{2,1,0:T(4,128)(2,1)} async-done(((bf16[64,3,2048]{2,1,0:T(4,128)(2,1)}), bf16[64,3,2048]{2,1,0:T(4,128)(2,1)}, u32[]{:S(2)}, u32[]{:S(2)}) %all-to-all-start.29) | async-done | bytes 786464 | tf_op jit(solution)/shard_map/all_to_all | solution.py:56
  1066.9 19.1 %all-to-all-done.30 = bf16[64,3,2048]{2,1,0:T(4,128)(2,1)} async-done(((bf16[64,3,2048]{2,1,0:T(4,128)(2,1)}), bf16[64,3,2048]{2,1,0:T(4,128)(2,1)}, u32[]{:S(2)}, u32[]{:S(2)}) %all-to-all-start.30) | async-done | bytes 786464 | tf_op jit(solution)/shard_map/all_to_all | solution.py:60
  1091.4 23.4 %collective-permute-done.10 = bf16[32,2048]{1,0:T(8,128)(2,1)S(1)} collective-permute-done((bf16[32,2048]{1,0:T(8,128)(2,1)S(1)}, bf16[32,2048]{1,0:T(8,128)(2,1)S(1)}, u32[]{:S(2)}, u32[]{:S(2)}) %collective-permute-start.10) | collective-permute-done | bytes 131104 | tf_op jit(solution)/shard_map/ppermute | solution.py:13
  1123.6 28.0 %all-to-all-done.31 = bf16[64,3,2048]{2,1,0:T(4,128)(2,1)} async-done(((bf16[64,3,2048]{2,1,0:T(4,128)(2,1)}), bf16[64,3,2048]{2,1,0:T(4,128)(2,1)}, u32[]{:S(2)}, u32[]{:S(2)}) %all-to-all-start.31) | async-done | bytes 786464 | tf_op jit(solution)/shard_map/all_to_all | solution.py:56
  1170.2 27.8 %all-to-all-done.32 = bf16[64,3,2048]{2,1,0:T(4,128)(2,1)} async-done(((bf16[64,3,2048]{2,1,0:T(4,128)(2,1)}), bf16[64,3,2048]{2,1,0:T(4,128)(2,1)}, u32[]{:S(2)}, u32[]{:S(2)}) %all-to-all-start.32) | async-done | bytes 786464 | tf_op jit(solution)/shard_map/all_to_all | solution.py:60
  1224.8 18.5 %all-to-all-done.33 = bf16[64,3,2048]{2,1,0:T(4,128)(2,1)} async-done(((bf16[64,3,2048]{2,1,0:T(4,128)(2,1)}), bf16[64,3,2048]{2,1,0:T(4,128)(2,1)}, u32[]{:S(2)}, u32[]{:S(2)}) %all-to-all-start.33) | async-done | bytes 786464 | tf_op jit(solution)/shard_map/all_to_all | solution.py:56
  1281.5 18.7 %all-to-all-done.34 = bf16[64,3,2048]{2,1,0:T(4,128)(2,1)S(1)} async-done(((bf16[64,3,2048]{2,1,0:T(4,128)(2,1)}), bf16[64,3,2048]{2,1,0:T(4,128)(2,1)S(1)}, u32[]{:S(2)}, u32[]{:S(2)}) %all-to-all-start.34) | async-done | bytes 786464 | tf_op jit(solution)/shard_map/all_to_all | solution.py:60
  1314.5 22.7 %psum.15 = f32[1,2048]{1,0:T(1,128)} all-reduce(f32[1,2048]{1,0:T(1,128)S(1)} %bitcast.633), channel_id=1, replica_groups=mesh['dp'=8,'pipe'=4,'expert'=8] {'dp'}, use_global_device_ids=true, to_apply=%region_85.86 | all-reduce | flops 2048 | bytes 16384 | tf_op jit(solution)/shard_map/psum | solution.py:228
  (409 shorter events, 699.8 us)
Async XLA Ops:
  5.5 27.2 %all-to-all-start = ((bf16[64,3,1]{1,2,0:T(2,128)(2,1)}), bf16[64,3,1]{1,2,0:T(2,128)(2,1)S(1)}, u32[]{:S(2)}, u32[]{:S(2)}) async-start(bf16[64,3,1]{1,2,0:T(2,128)(2,1)} %copy.214), calls=%async_computation | async-start | bytes 65536 | tf_op jit(solution)/shard_map/all_to_all | solution.py:46
  32.7 33.2 %all-to-all-start.1 = ((bf16[64,3,2048]{2,1,0:T(4,128)(2,1)}), bf16[64,3,2048]{2,1,0:T(4,128)(2,1)}, u32[]{:S(2)}, u32[]{:S(2)}) async-start(bf16[64,3,2048]{2,1,0:T(4,128)(2,1)} %copy.215), calls=%async_computation.1 | async-start | bytes 2097152 | tf_op jit(solution)/shard_map/all_to_all | solution.py:45
  78.3 24.5 %all-to-all-start.2 = ((bf16[64,3,2048]{2,1,0:T(4,128)(2,1)}), bf16[64,3,2048]{2,1,0:T(4,128)(2,1)}, u32[]{:S(2)}, u32[]{:S(2)}) async-start(bf16[64,3,2048]{2,1,0:T(4,128)(2,1)} %reshape.639), calls=%async_computation.2 | async-start | bytes 2097152 | tf_op jit(solution)/shard_map/all_to_all | solution.py:52
  122.4 43.0 %all-to-all-start.4 = ((bf16[64,3,2048]{2,1,0:T(4,128)(2,1)}), bf16[64,3,2048]{2,1,0:T(4,128)(2,1)}, u32[]{:S(2)}, u32[]{:S(2)}) async-start(bf16[64,3,2048]{2,1,0:T(4,128)(2,1)} %copy.219), calls=%async_computation.4 | async-start | bytes 2097152 | tf_op jit(solution)/shard_map/all_to_all | solution.py:45
  178.0 24.5 %all-to-all-start.5 = ((bf16[64,3,2048]{2,1,0:T(4,128)(2,1)}), bf16[64,3,2048]{2,1,0:T(4,128)(2,1)}, u32[]{:S(2)}, u32[]{:S(2)}) async-start(bf16[64,3,2048]{2,1,0:T(4,128)(2,1)} %reshape.641), calls=%async_computation.5 | async-start | bytes 2097152 | tf_op jit(solution)/shard_map/all_to_all | solution.py:52
  205.4 23.7 %collective-permute-start.1 = (bf16[32,2048]{1,0:T(8,128)(2,1)S(1)}, bf16[32,2048]{1,0:T(8,128)(2,1)S(1)}, u32[]{:S(2)}, u32[]{:S(2)}) collective-permute-start(bf16[32,2048]{1,0:T(8,128)(2,1)S(1)} %get-tuple-element.841), channel_id=1, source_target_pairs={{0,8},{8,16},{16,24},{1,9},{9,17},{17,25},{2,10},{10,18},{18,26},{... | collective-permute-start | bytes 393224 | tf_op jit(solution)/shard_map/ppermute | solution.py:13
  240.8 34.5 %all-to-all-start.7 = ((bf16[64,3,2048]{2,1,0:T(4,128)(2,1)}), bf16[64,3,2048]{2,1,0:T(4,128)(2,1)}, u32[]{:S(2)}, u32[]{:S(2)}) async-start(bf16[64,3,2048]{2,1,0:T(4,128)(2,1)} %copy.223), calls=%async_computation.7 | async-start | bytes 2097152 | tf_op jit(solution)/shard_map/all_to_all | solution.py:45
  287.7 31.1 %all-to-all-start.8 = ((bf16[64,3,2048]{2,1,0:T(4,128)(2,1)}), bf16[64,3,2048]{2,1,0:T(4,128)(2,1)}, u32[]{:S(2)}, u32[]{:S(2)}) async-start(bf16[64,3,2048]{2,1,0:T(4,128)(2,1)} %reshape.643), calls=%async_computation.8 | async-start | bytes 2097152 | tf_op jit(solution)/shard_map/all_to_all | solution.py:52
  324.2 20.9 %all-to-all-start.9 = ((bf16[64,3,1]{1,2,0:T(2,128)(2,1)}), bf16[64,3,1]{1,2,0:T(2,128)(2,1)S(1)}, u32[]{:S(2)}, u32[]{:S(2)}) async-start(bf16[64,3,1]{1,2,0:T(2,128)(2,1)} %copy.226), calls=%async_computation.9 | async-start | bytes 65536 | tf_op jit(solution)/shard_map/all_to_all | solution.py:46
  345.1 32.7 %all-to-all-start.10 = ((bf16[64,3,2048]{2,1,0:T(4,128)(2,1)}), bf16[64,3,2048]{2,1,0:T(4,128)(2,1)}, u32[]{:S(2)}, u32[]{:S(2)}) async-start(bf16[64,3,2048]{2,1,0:T(4,128)(2,1)} %copy.227), calls=%async_computation.10 | async-start | bytes 2097152 | tf_op jit(solution)/shard_map/all_to_all | solution.py:45
  390.2 31.1 %all-to-all-start.11 = ((bf16[64,3,2048]{2,1,0:T(4,128)(2,1)}), bf16[64,3,2048]{2,1,0:T(4,128)(2,1)}, u32[]{:S(2)}, u32[]{:S(2)}) async-start(bf16[64,3,2048]{2,1,0:T(4,128)(2,1)} %reshape.645), calls=%async_computation.11 | async-start | bytes 2097152 | tf_op jit(solution)/shard_map/all_to_all | solution.py:52
  447.0 27.6 %all-to-all-start.13 = ((bf16[64,3,2048]{2,1,0:T(4,128)(2,1)}), bf16[64,3,2048]{2,1,0:T(4,128)(2,1)}, u32[]{:S(2)}, u32[]{:S(2)}) async-start(bf16[64,3,2048]{2,1,0:T(4,128)(2,1)} %copy.231), calls=%async_computation.13 | async-start | bytes 2097152 | tf_op jit(solution)/shard_map/all_to_all | solution.py:45
  479.9 30.7 %all-to-all-start.14 = ((bf16[64,3,2048]{2,1,0:T(4,128)(2,1)}), bf16[64,3,2048]{2,1,0:T(4,128)(2,1)}, u32[]{:S(2)}, u32[]{:S(2)}) async-start(bf16[64,3,2048]{2,1,0:T(4,128)(2,1)} %reshape.647), calls=%async_computation.14 | async-start | bytes 2097152 | tf_op jit(solution)/shard_map/all_to_all | solution.py:52
  536.3 28.2 %all-to-all-start.16 = ((bf16[64,3,2048]{2,1,0:T(4,128)(2,1)}), bf16[64,3,2048]{2,1,0:T(4,128)(2,1)}, u32[]{:S(2)}, u32[]{:S(2)}) async-start(bf16[64,3,2048]{2,1,0:T(4,128)(2,1)} %copy.235), calls=%async_computation.16 | async-start | bytes 2097152 | tf_op jit(solution)/shard_map/all_to_all | solution.py:45
  569.6 37.7 %all-to-all-start.17 = ((bf16[64,3,2048]{2,1,0:T(4,128)(2,1)}), bf16[64,3,2048]{2,1,0:T(4,128)(2,1)}, u32[]{:S(2)}, u32[]{:S(2)}) async-start(bf16[64,3,2048]{2,1,0:T(4,128)(2,1)} %reshape.649), calls=%async_computation.17 | async-start | bytes 2097152 | tf_op jit(solution)/shard_map/all_to_all | solution.py:52
  631.6 34.4 %all-to-all-start.19 = ((bf16[64,3,2048]{2,1,0:T(4,128)(2,1)}), bf16[64,3,2048]{2,1,0:T(4,128)(2,1)}, u32[]{:S(2)}, u32[]{:S(2)}) async-start(bf16[64,3,2048]{2,1,0:T(4,128)(2,1)} %copy.239), calls=%async_computation.19 | async-start | bytes 2097152 | tf_op jit(solution)/shard_map/all_to_all | solution.py:45
  666.0 24.4 %all-to-all-start.21 = ((bf16[64,3,2048]{2,1,0:T(4,128)(2,1)}), bf16[64,3,2048]{2,1,0:T(4,128)(2,1)}, u32[]{:S(2)}, u32[]{:S(2)}) async-start(bf16[64,3,2048]{2,1,0:T(4,128)(2,1)} %copy.242), calls=%async_computation.21 | async-start | bytes 2097152 | tf_op jit(solution)/shard_map/all_to_all | solution.py:56
  694.6 27.6 %all-to-all-start.22 = ((bf16[64,3,2048]{2,1,0:T(4,128)(2,1)}), bf16[64,3,2048]{2,1,0:T(4,128)(2,1)}, u32[]{:S(2)}, u32[]{:S(2)}) async-start(bf16[64,3,2048]{2,1,0:T(4,128)(2,1)} %reshape.654), calls=%async_computation.22 | async-start | bytes 2097152 | tf_op jit(solution)/shard_map/all_to_all | solution.py:60
  744.6 34.2 %all-to-all-start.23 = ((bf16[64,3,2048]{2,1,0:T(4,128)(2,1)}), bf16[64,3,2048]{2,1,0:T(4,128)(2,1)}, u32[]{:S(2)}, u32[]{:S(2)}) async-start(bf16[64,3,2048]{2,1,0:T(4,128)(2,1)} %copy.251), calls=%async_computation.23 | async-start | bytes 2097152 | tf_op jit(solution)/shard_map/all_to_all | solution.py:56
  783.1 24.3 %all-to-all-start.24 = ((bf16[64,3,2048]{2,1,0:T(4,128)(2,1)}), bf16[64,3,2048]{2,1,0:T(4,128)(2,1)}, u32[]{:S(2)}, u32[]{:S(2)}) async-start(bf16[64,3,2048]{2,1,0:T(4,128)(2,1)} %reshape.656), calls=%async_computation.24 | async-start | bytes 2097152 | tf_op jit(solution)/shard_map/all_to_all | solution.py:60
  827.4 40.7 %all-to-all-start.25 = ((bf16[64,3,2048]{2,1,0:T(4,128)(2,1)}), bf16[64,3,2048]{2,1,0:T(4,128)(2,1)}, u32[]{:S(2)}, u32[]{:S(2)}) async-start(bf16[64,3,2048]{2,1,0:T(4,128)(2,1)} %copy.253), calls=%async_computation.25 | async-start | bytes 2097152 | tf_op jit(solution)/shard_map/all_to_all | solution.py:56
  872.5 24.3 %all-to-all-start.26 = ((bf16[64,3,2048]{2,1,0:T(4,128)(2,1)}), bf16[64,3,2048]{2,1,0:T(4,128)(2,1)}, u32[]{:S(2)}, u32[]{:S(2)}) async-start(bf16[64,3,2048]{2,1,0:T(4,128)(2,1)} %reshape.658), calls=%async_computation.26 | async-start | bytes 2097152 | tf_op jit(solution)/shard_map/all_to_all | solution.py:60
  922.4 36.3 %all-to-all-start.27 = ((bf16[64,3,2048]{2,1,0:T(4,128)(2,1)}), bf16[64,3,2048]{2,1,0:T(4,128)(2,1)}, u32[]{:S(2)}, u32[]{:S(2)}) async-start(bf16[64,3,2048]{2,1,0:T(4,128)(2,1)} %copy.255), calls=%async_computation.27 | async-start | bytes 2097152 | tf_op jit(solution)/shard_map/all_to_all | solution.py:56
  971.6 24.4 %all-to-all-start.28 = ((bf16[64,3,2048]{2,1,0:T(4,128)(2,1)}), bf16[64,3,2048]{2,1,0:T(4,128)(2,1)}, u32[]{:S(2)}, u32[]{:S(2)}) async-start(bf16[64,3,2048]{2,1,0:T(4,128)(2,1)} %reshape.660), calls=%async_computation.28 | async-start | bytes 2097152 | tf_op jit(solution)/shard_map/all_to_all | solution.py:60
  1012.4 36.3 %all-to-all-start.29 = ((bf16[64,3,2048]{2,1,0:T(4,128)(2,1)}), bf16[64,3,2048]{2,1,0:T(4,128)(2,1)}, u32[]{:S(2)}, u32[]{:S(2)}) async-start(bf16[64,3,2048]{2,1,0:T(4,128)(2,1)} %copy.257), calls=%async_computation.29 | async-start | bytes 2097152 | tf_op jit(solution)/shard_map/all_to_all | solution.py:56
  1061.6 24.4 %all-to-all-start.30 = ((bf16[64,3,2048]{2,1,0:T(4,128)(2,1)}), bf16[64,3,2048]{2,1,0:T(4,128)(2,1)}, u32[]{:S(2)}, u32[]{:S(2)}) async-start(bf16[64,3,2048]{2,1,0:T(4,128)(2,1)} %reshape.662), calls=%async_computation.30 | async-start | bytes 2097152 | tf_op jit(solution)/shard_map/all_to_all | solution.py:60
  1090.1 24.7 %collective-permute-start.10 = (bf16[32,2048]{1,0:T(8,128)(2,1)S(1)}, bf16[32,2048]{1,0:T(8,128)(2,1)S(1)}, u32[]{:S(2)}, u32[]{:S(2)}) collective-permute-start(bf16[32,2048]{1,0:T(8,128)(2,1)S(1)} %get-tuple-element.782), channel_id=1, source_target_pairs={{8,0},{16,8},{24,16},{9,1},{17,9},{25,17},{10,2},{18,10},{26,18},{... | collective-permute-start | bytes 393224 | tf_op jit(solution)/shard_map/ppermute | solution.py:13
  1117.9 33.7 %all-to-all-start.31 = ((bf16[64,3,2048]{2,1,0:T(4,128)(2,1)}), bf16[64,3,2048]{2,1,0:T(4,128)(2,1)}, u32[]{:S(2)}, u32[]{:S(2)}) async-start(bf16[64,3,2048]{2,1,0:T(4,128)(2,1)} %copy.259), calls=%async_computation.31 | async-start | bytes 2097152 | tf_op jit(solution)/shard_map/all_to_all | solution.py:56
  1164.6 33.5 %all-to-all-start.32 = ((bf16[64,3,2048]{2,1,0:T(4,128)(2,1)}), bf16[64,3,2048]{2,1,0:T(4,128)(2,1)}, u32[]{:S(2)}, u32[]{:S(2)}) async-start(bf16[64,3,2048]{2,1,0:T(4,128)(2,1)} %reshape.664), calls=%async_computation.32 | async-start | bytes 2097152 | tf_op jit(solution)/shard_map/all_to_all | solution.py:60
  1211.5 31.9 %all-to-all-start.33 = ((bf16[64,3,2048]{2,1,0:T(4,128)(2,1)}), bf16[64,3,2048]{2,1,0:T(4,128)(2,1)}, u32[]{:S(2)}, u32[]{:S(2)}) async-start(bf16[64,3,2048]{2,1,0:T(4,128)(2,1)} %copy.261), calls=%async_computation.33 | async-start | bytes 2097152 | tf_op jit(solution)/shard_map/all_to_all | solution.py:56
  1243.3 29.7 %all-to-all-start.20 = ((bf16[64,3,2048]{2,1,0:T(4,128)(2,1)}), bf16[64,3,2048]{2,1,0:T(4,128)(2,1)}, u32[]{:S(2)}, u32[]{:S(2)}) async-start(bf16[64,3,2048]{2,1,0:T(4,128)(2,1)} %reshape.651), calls=%async_computation.20 | async-start | bytes 2097152 | tf_op jit(solution)/shard_map/all_to_all | solution.py:52
  1273.1 27.1 %all-to-all-start.34 = ((bf16[64,3,2048]{2,1,0:T(4,128)(2,1)}), bf16[64,3,2048]{2,1,0:T(4,128)(2,1)S(1)}, u32[]{:S(2)}, u32[]{:S(2)}) async-start(bf16[64,3,2048]{2,1,0:T(4,128)(2,1)} %reshape.666), calls=%async_computation.34 | async-start | bytes 2097152 | tf_op jit(solution)/shard_map/all_to_all | solution.py:60
  (43 other events, 477.0 us)
